TPU v7x, 32 devices: a whole 2x2x4 slice. The times are simulated.
32 devices in a mesh: gx: 4 (over y, x), gy: 4 (over z), gz: 2 (over core).
Axes of the slice: x: 2, y: 2, z: 4, core: 2. Of those that a mesh axis runs over, the one named last changes fastest.
Arguments:
- viscosity: float32 [128, 64, 256], P('gx', 'gy', 'gz'), may hold values from 0.001 to 1000
- force: float32 [3, 128, 64, 256], P(None, 'gx', 'gy', 'gz'), may hold values from -6 to 6
Outputs:
- solution: float32 [4, 128, 64, 256], P(None, 'gx', 'gy', 'gz')
- residual: float32 [4, 128, 64, 256], P(None, 'gx', 'gy', 'gz')
All inputs are finite; a program needn't handle non-finite values.
Results may differ from a plain program's by a relative error of at most 0.0003.
Values sent between devices are 32-bit elements; how exact they have to be, the bound alone decides.
A program may use at most 128 MiB of HBM per device.

v0:
```python
import functools
import jax
import jax.numpy as jnp
from jax import lax
from jax.experimental import pallas as pl
from jax.experimental.pallas import tpu as pltpu
from jax.sharding import PartitionSpec as P

MESH = pl.DeviceIdType.MESH
AXES = ("gx", "gy", "gz")
SWEEPS = 3
LOW, HIGH = 0.25, 2.0
ROUNDS = 9
WIDTHS = (1, 3, 3, 3, 3, 4, 3, 3, 3)
UNROLL = 4


def cheb_constants():
    mid, half = 0.5 * (HIGH + LOW), 0.5 * (HIGH - LOW)
    s = mid / half
    rho = 1.0 / s
    steps = []
    for _ in range(SWEEPS):
        nxt = 1.0 / (2.0 * s - rho)
        steps.append((nxt * rho, 2.0 * nxt / half))
        rho = nxt
    return mid, steps


def kernel(counts, chunks, eta_hbm, force_hbm, sol_hbm, res_hbm,
           e_ref, b_ref, f_ref, cx_ref, cym_ref, cyp_ref, czm_ref, czp_ref, dg_ref, inv_ref,
           r_ref, x_ref, w0_ref, w1_ref, so_ref, ro_ref,
           sy_ref, hy_ref, sz_ref, hz_ref, ar_ref,
           in_sem, out_sem, xs_sem, xr_sem, ys_sem, yr_sem, zs_sem, zr_sem, as_sem, ar_sem):
    X, Y, Z = b_ref.shape[1:]
    mid, steps = cheb_constants()
    me = [lax.axis_index(a) for a in AXES]
    nch = len(chunks)
    order = [0] + ([nch - 1] if nch > 1 else []) + list(range(1, nch - 1))

    load_e = pltpu.make_async_copy(eta_hbm, e_ref.at[0, pl.ds(1, X)], in_sem.at[0])
    load_b = pltpu.make_async_copy(force_hbm, b_ref, in_sem.at[1])
    load_e.start()
    load_b.start()

    def device(dim, index):
        spot = list(me)
        spot[dim] = index
        return tuple(spot)

    barrier = pltpu.get_barrier_semaphore()
    for dim in range(3):
        for off in range(1, counts[dim]):
            pl.semaphore_signal(barrier, inc=1, device_id=device(dim, lax.rem(me[dim] + off, counts[dim])),
                                device_id_type=MESH)

    def field(k):
        return e_ref if k == 0 else f_ref.at[k - 1]

    def target(dim, side):
        return device(dim, me[dim] + (1 if side == 0 else -1))

    def sends(dim, side):
        return me[dim] < counts[dim] - 1 if side == 0 else me[dim] > 0

    def receives(dim, side):
        return me[dim] > 0 if side == 0 else me[dim] < counts[dim] - 1

    def x_copy(k, side):
        n = WIDTHS[k]
        face, halo = (X, 0) if side == 0 else (1, X + 1)
        return pltpu.make_async_remote_copy(
            src_ref=field(k).at[pl.ds(0, n), face], dst_ref=field(k).at[pl.ds(0, n), halo],
            send_sem=xs_sem.at[k, side], recv_sem=xr_sem.at[k, side],
            device_id=target(0, side), device_id_type=MESH)

    def y_copy(k, side, ch):
        n = WIDTHS[k]
        lo, hi = chunks[ch]
        return pltpu.make_async_remote_copy(
            src_ref=sy_ref.at[k, side, pl.ds(0, n), pl.ds(lo, hi - lo)],
            dst_ref=hy_ref.at[k, side, pl.ds(0, n), pl.ds(lo, hi - lo)],
            send_sem=ys_sem.at[k, side, ch], recv_sem=yr_sem.at[k, side, ch],
            device_id=target(1, side), device_id_type=MESH)

    def z_copy(k, side, ch):
        return pltpu.make_async_remote_copy(
            src_ref=sz_ref.at[k, side, ch], dst_ref=hz_ref.at[k, side, ch],
            send_sem=zs_sem.at[k, side, ch], recv_sem=zr_sem.at[k, side, ch],
            device_id=target(2, side), device_id_type=MESH)

    def start_chunk(k, ch):
        for side in (0, 1):
            @pl.when(sends(1, side))
            def _():
                y_copy(k, side, ch).start()
            @pl.when(sends(2, side))
            def _():
                z_copy(k, side, ch).start()
        for side, edge in ((0, nch - 1), (1, 0)):
            if ch == edge:
                @pl.when(sends(0, side))
                def _():
                    x_copy(k, side).start()

    def wait_chunk(k, ch):
        for side in (0, 1):
            @pl.when(receives(1, side))
            def _():
                y_copy(k, side, ch).wait_recv()
            @pl.when(receives(2, side))
            def _():
                z_copy(k, side, ch).wait_recv()
        for side, edge in ((0, 0), (1, nch - 1)):
            if ch == edge:
                @pl.when(receives(0, side))
                def _():
                    x_copy(k, side).wait_recv()

    for side in (0, 1):
        @pl.when(jnp.logical_not(receives(0, side)))
        def _():
            zero = jnp.zeros((Y, Z), jnp.float32)
            for k in range(ROUNDS):
                for c in range(WIDTHS[k]):
                    field(k)[c, 0 if side == 0 else X + 1] = zero
        @pl.when(jnp.logical_not(receives(1, side)))
        def _():
            def body(k, carry):
                hy_ref[k, side] = jnp.zeros(hy_ref.shape[2:], jnp.float32)
                return carry
            lax.fori_loop(0, ROUNDS, body, 0)
        @pl.when(jnp.logical_not(receives(2, side)))
        def _():
            def body(k, carry):
                hz_ref[k, side] = jnp.zeros(hz_ref.shape[2:], jnp.float32)
                return carry
            lax.fori_loop(0, ROUNDS, body, 0)

    row = lax.broadcasted_iota(jnp.int32, (Y, Z), 0)
    lane = lax.broadcasted_iota(jnp.int32, (Y, Z), 1)
    blank = jnp.zeros((Y, Z), jnp.float32)
    first_row, last_row, first_lane, last_lane = row == 0, row == Y - 1, lane == 0, lane == Z - 1

    def neighbours(k, ch, c, x):
        f = field(k)
        u = f[c, x + 1]
        spot = c * X + x
        ym = jnp.where(first_row, hy_ref[k, 0, c, pl.ds(x, 1)], pltpu.roll(u, 1, 0))
        yp = jnp.where(last_row, hy_ref[k, 1, c, pl.ds(x, 1)], pltpu.roll(u, Y - 1, 0))
        zm = jnp.where(first_lane, pltpu.roll(hz_ref[k, 0, ch], lax.rem(Z - spot, Z), 1), pltpu.roll(u, 1, 1))
        zp = jnp.where(last_lane, pltpu.roll(hz_ref[k, 1, ch], Z - 1 - spot, 1), pltpu.roll(u, Z - 1, 1))
        return u, f[c, x], f[c, x + 2], ym, yp, zm, zp

    def put(k, c, x, value, packs, store=True):
        if store:
            field(k)[c, x + 1] = value
        sy_ref[k, 0, c, pl.ds(x, 1)] = value[Y - 1:Y]
        sy_ref[k, 1, c, pl.ds(x, 1)] = value[0:1]
        here = lane == c * X + x
        return (jnp.where(here, jnp.broadcast_to(value[:, Z - 1:Z], (Y, Z)), packs[0]),
                jnp.where(here, jnp.broadcast_to(value[:, 0:1], (Y, Z)), packs[1]))

    def sweep(need, make, body, extra=()):
        for ch in order:
            if need is not None:
                wait_chunk(need, ch)
            lo, hi = chunks[ch]
            def step(x, carry):
                return body(ch, x, carry[0], carry[1])
            packs, extra = lax.fori_loop(lo, hi, step, ((blank, blank), extra), unroll=UNROLL)
            if make is not None:
                sz_ref[make, 0, ch] = packs[0]
                sz_ref[make, 1, ch] = packs[1]
                start_chunk(make, ch)
        return extra

    load_e.wait()
    pl.semaphore_wait(barrier, sum(counts) - 3)
    sweep(None, 0, lambda ch, x, packs, extra: (put(0, 0, x, e_ref[0, x + 1], packs, False), extra))
    load_b.wait()

    def setup(ch, x, packs, extra):
        u, xm, xp, ym, yp, zm, zp = neighbours(0, ch, 0, x)
        cxm, cxp = 0.5 * (u + xm), 0.5 * (u + xp)
        cym, cyp = 0.5 * (u + ym), 0.5 * (u + yp)
        czm, czp = 0.5 * (u + zm), 0.5 * (u + zp)
        cx_ref[x] = cxm
        cx_ref[x + 1] = cxp
        cym_ref[x], cyp_ref[x], czm_ref[x], czp_ref[x] = cym, cyp, czm, czp
        diagonal = cxp + cxm + cyp + cym + czp + czm
        inverse = 1.0 / diagonal
        dg_ref[x] = diagonal
        inv_ref[x] = inverse
        for c in range(3):
            packs = put(1, c, x, b_ref[c, x] * inverse / mid, packs)
        return packs, extra

    sweep(0, 1, setup)

    def viscous(near, coef):
        u, xm, xp, ym, yp, zm, zp = near
        cxm, cxp, cym, cyp, czm, czp, dg = coef
        return dg * u - cxp * xp - cxm * xm - cyp * yp - cym * ym - czp * zp - czm * zm

    def coefs(x):
        return (cx_ref[x], cx_ref[x + 1], cym_ref[x], cyp_ref[x], czm_ref[x], czp_ref[x], dg_ref[x])

    def smooth(base, forcing, at, shift=None):
        keep, gain = steps[at]
        src, dst = base + at, base + at + 1
        last = at == SWEEPS - 1

        def body(ch, x, packs, extra):
            coef, inverse = coefs(x), inv_ref[x]
            for c in range(3):
                near = neighbours(src, ch, c, x)
                r = (forcing[c, x] if at == 0 else r_ref[c, x]) - viscous(near, coef)
                d = keep * near[0] + gain * r * inverse
                total = (near[0] if at == 0 else x_ref[c, x]) + d
                if last:
                    if shift is not None:
                        total = total - shift * f_ref[base - 2, c, x + 1]
                    packs = put(dst, c, x, total, packs)
                else:
                    r_ref[c, x] = r
                    x_ref[c, x] = total
                    packs = put(dst, c, x, d, packs)
            return packs, extra

        sweep(src, dst, body)

    stages = (2, 0, 1)
    starts = [sum(counts[d] for d in stages[:i]) for i in range(3)]

    def ar_copy(which, stage, off):
        dim = stages[stage]
        slot = starts[stage] + me[dim]
        peer = lax.rem(me[dim] + off, counts[dim])
        return pltpu.make_async_remote_copy(
            src_ref=ar_ref.at[which, slot], dst_ref=ar_ref.at[which, slot],
            send_sem=as_sem.at[which, starts[stage] + off], recv_sem=ar_sem.at[which, slot],
            device_id=device(dim, peer), device_id_type=MESH)

    def ar_start(which, stage, tile):
        dim = stages[stage]
        ar_ref[which, starts[stage] + me[dim]] = tile
        for off in range(1, counts[dim]):
            ar_copy(which, stage, off).start()

    def ar_wait(which, stage):
        dim = stages[stage]
        for off in range(1, counts[dim]):
            slot = starts[stage] + lax.rem(me[dim] + off, counts[dim])
            pltpu.make_async_remote_copy(
                src_ref=ar_ref.at[which, slot], dst_ref=ar_ref.at[which, slot],
                send_sem=as_sem.at[which, starts[stage] + off], recv_sem=ar_sem.at[which, slot],
                device_id=device(dim, lax.rem(me[dim] + off, counts[dim])), device_id_type=MESH).wait_recv()
        total = ar_ref[which, starts[stage]]
        for i in range(1, counts[dim]):
            total = total + ar_ref[which, starts[stage] + i]
        return total

    rows8 = lax.broadcasted_iota(jnp.int32, (8, Z), 0)

    def tile_of(sums):
        tile = jnp.zeros((8, Z), jnp.float32)
        for i, s in enumerate(sums):
            tile = jnp.where(rows8 == i, jnp.sum(s, axis=0, keepdims=True), tile)
        return tile

    def totals(tile, n):
        whole = jnp.broadcast_to(jnp.sum(tile, axis=1, keepdims=True), (8, Z))
        return [whole[i:i + 1] for i in range(n)]

    for at in range(SWEEPS):
        smooth(1, b_ref, at)

    def stokes0(ch, x, packs, sums):
        bb, wb, ww = sums
        coef, inverse = coefs(x), inv_ref[x]
        near = [neighbours(4, ch, c, x) for c in range(3)]
        for c in range(3):
            w, b = viscous(near[c], coef), b_ref[c, x]
            bb, wb, ww = bb + b * b, wb + w * b, ww + w * w
            w0_ref[c, x] = w
            packs = put(5, c, x, w * inverse / mid, packs)
        div = -0.5 * (near[0][2] - near[0][1] + (near[1][4] - near[1][3]) + (near[2][6] - near[2][5]))
        ww = ww + div * div
        w0_ref[3, x] = div
        packs = put(5, 3, x, e_ref[0, x + 1] * div, packs)
        return packs, (bb, wb, ww)

    sums = sweep(4, 5, stokes0, (blank, blank, blank))
    ar_start(0, 0, tile_of(sums))

    smooth(5, w0_ref, 0)
    ar_start(0, 1, ar_wait(0, 0))
    smooth(5, w0_ref, 1)
    ar_start(0, 2, ar_wait(0, 1))
    square, wb, ww = totals(ar_wait(0, 2), 3)
    h00 = wb / square
    h10 = jnp.sqrt(ww / square - h00 * h00)
    smooth(5, w0_ref, 2, h00)

    def stokes1(ch, x, packs, sums):
        wb, wu, ww = sums
        coef = coefs(x)
        near = [neighbours(8, ch, c, x) for c in range(3)]
        _, pxm, pxp, pym, pyp, pzm, pzp = neighbours(5, ch, 3, x)
        grads = (0.5 * (pxp - pxm), 0.5 * (pyp - pym), 0.5 * (pzp - pzm))
        for c in range(3):
            w, b = viscous(near[c], coef) + grads[c], b_ref[c, x]
            u = w0_ref[c, x] - h00 * b
            wb, wu, ww = wb + w * b, wu + w * u, ww + w * w
            w1_ref[c, x] = w
        div = -0.5 * (near[0][2] - near[0][1] + (near[1][4] - near[1][3]) + (near[2][6] - near[2][5]))
        wu, ww = wu + div * w0_ref[3, x], ww + div * div
        w1_ref[3, x] = div
        return packs, (wb, wu, ww)

    sums = sweep(8, None, stokes1, (blank, blank, blank))
    ar_start(1, 0, tile_of(sums))
    ar_start(1, 1, ar_wait(1, 0))
    ar_start(1, 2, ar_wait(1, 1))
    wb, wu, ww = totals(ar_wait(1, 2), 3)

    beta = jnp.sqrt(square)
    h01 = wb / (square * h10)
    h11 = wu / (square * h10 * h10)
    h21 = jnp.sqrt(ww / (square * h10 * h10) - h01 * h01 - h11 * h11)
    n00, n01, n11 = h00 * h00 + h10 * h10, h00 * h01 + h10 * h11, h01 * h01 + h11 * h11 + h21 * h21
    l00 = jnp.sqrt(n00)
    l10 = n01 / l00
    l11 = jnp.sqrt(n11 - l10 * l10)
    g0 = beta * h00 / l00
    g1 = (beta * h01 - l10 * g0) / l11
    y1 = g1 / l11
    y0 = (g0 - l10 * y1) / l00
    c0 = beta - (h00 * y0 + h01 * y1)
    c1 = -(h10 * y0 + h11 * y1)
    c2 = -(h21 * y1)
    z0_weight, z1_weight = y0 / beta, y1 / (beta * h10)
    b_weight = (c0 - c2 * h01 / h21) / beta
    u_weight = (c1 - c2 * h11 / h21) / (beta * h10)
    w_weight = c2 / (h21 * beta * h10)

    def out_copies(ch):
        lo, hi = chunks[ch]
        span = pl.ds(lo, hi - lo)
        return (pltpu.make_async_copy(so_ref.at[:, span], sol_hbm.at[:, span], out_sem.at[0, ch]),
                pltpu.make_async_copy(ro_ref.at[:, span], res_hbm.at[:, span], out_sem.at[1, ch]))

    for ch in range(nch):
        def body(x, carry):
            for c in range(3):
                b = b_ref[c, x]
                so_ref[c, x] = z0_weight * f_ref[3, c, x + 1] + z1_weight * f_ref[7, c, x + 1]
                ro_ref[c, x] = b_weight * b + u_weight * (w0_ref[c, x] - h00 * b) + w_weight * w1_ref[c, x]
            so_ref[3, x] = z1_weight * f_ref[4, 3, x + 1]
            ro_ref[3, x] = u_weight * w0_ref[3, x] + w_weight * w1_ref[3, x]
            return carry
        lax.fori_loop(*chunks[ch], body, 0, unroll=UNROLL)
        for copy in out_copies(ch):
            copy.start()

    for side in (0, 1):
        @pl.when(sends(0, side))
        def _():
            for k in range(ROUNDS):
                x_copy(k, side).wait_send()
        @pl.when(sends(1, side))
        def _():
            for k in range(ROUNDS):
                for ch in range(nch):
                    y_copy(k, side, ch).wait_send()
        @pl.when(sends(2, side))
        def _():
            for k in range(ROUNDS):
                for ch in range(nch):
                    z_copy(k, side, ch).wait_send()
    for which in (0, 1):
        for stage in range(3):
            for off in range(1, counts[stages[stage]]):
                ar_copy(which, stage, off).wait_send()
    for ch in range(nch):
        for copy in out_copies(ch):
            copy.wait()


def solution(mesh):
    counts = tuple(mesh.shape[a] for a in AXES)

    def shards(viscosity, force):
        X, Y, Z = viscosity.shape
        assert 4 * X <= Z
        size = 8 if X % 8 == 0 else X
        chunks = tuple((lo, lo + size) for lo in range(0, X, size))
        nch = len(chunks)
        f32 = jnp.float32
        block = pltpu.VMEM((X, Y, Z), f32)
        dma = pltpu.SemaphoreType.DMA
        spots = sum(counts)
        scratch = [
            pltpu.VMEM((1, X + 2, Y, Z), f32), pltpu.VMEM((3, X, Y, Z), f32),
            pltpu.VMEM((ROUNDS - 1, 4, X + 2, Y, Z), f32), pltpu.VMEM((X + 1, Y, Z), f32),
            block, block, block, block, block, block,
            pltpu.VMEM((3, X, Y, Z), f32), pltpu.VMEM((3, X, Y, Z), f32),
            pltpu.VMEM((4, X, Y, Z), f32), pltpu.VMEM((4, X, Y, Z), f32),
            pltpu.VMEM((4, X, Y, Z), f32), pltpu.VMEM((4, X, Y, Z), f32),
            pltpu.VMEM((ROUNDS, 2, 4, X, Z), f32), pltpu.VMEM((ROUNDS, 2, 4, X, Z), f32),
            pltpu.VMEM((ROUNDS, 2, nch, Y, Z), f32), pltpu.VMEM((ROUNDS, 2, nch, Y, Z), f32),
            pltpu.VMEM((2, spots, 8, Z), f32),
            dma((2,)), dma((2, nch)), dma((ROUNDS, 2)), dma((ROUNDS, 2)),
            dma((ROUNDS, 2, nch)), dma((ROUNDS, 2, nch)), dma((ROUNDS, 2, nch)), dma((ROUNDS, 2, nch)),
            dma((2, spots)), dma((2, spots)),
        ]
        anywhere = pl.BlockSpec(memory_space=pl.ANY)
        out = jax.ShapeDtypeStruct((4, X, Y, Z), f32)
        return tuple(pl.pallas_call(
            functools.partial(kernel, counts, chunks),
            out_shape=(out, out),
            in_specs=[anywhere, anywhere],
            out_specs=(anywhere, anywhere),
            scratch_shapes=scratch,
            name="fgmres",
            compiler_params=pltpu.CompilerParams(
                collective_id=0, has_side_effects=True, vmem_limit_bytes=56 * 1024 * 1024),
        )(viscosity, force))

    return jax.shard_map(
        shards,
        mesh=mesh,
        in_specs=(P("gx", "gy", "gz"), P(None, "gx", "gy", "gz")),
        out_specs=(P(None, "gx", "gy", "gz"), P(None, "gx", "gy", "gz")),
        check_vma=False,
    )
```

profile of v0, /device:TPU:0, one launch (start us, length us, event | category | flops | bytes accessed | tf_op | source)
XLA Modules:
  0.0 63.6 jit_solution(4593610131161271991)
XLA Ops:
  0.6 59.6 %fgmres.1 = (f32[4,32,16,128]{3,2,1,0:T(8,128)}, f32[4,32,16,128]{3,2,1,0:T(8,128)}) custom-call(f32[32,16,128]{2,1,0:T(8,128)} %eta_hbm.1, f32[3,32,16,128]{3,2,1,0:T(8,128)} %force_hbm.1), custom_call_target="tpu_custom_call" | custom-call | tf_op jit(solution)/shard_map/fgmres/pallas_call | solution.py:420
  60.2 0.0 copy-start
  60.3 2.4 %copy.6 = f32[4,32,16,128]{3,2,1,0:T(8,128)} copy(f32[4,32,16,128]{3,2,1,0:T(8,128)} %get-tuple-element.4) | data formatting | bytes 2097152
  62.6 0.0 copy-done
  62.6 1.0 %copy.7 = f32[4,32,16,128]{3,2,1,0:T(8,128)} copy(f32[4,32,16,128]{3,2,1,0:T(8,128)S(1)} %copy-done) | data formatting | bytes 2097152
Async XLA Ops:
  60.2 2.4 %copy-start = (f32[4,32,16,128]{3,2,1,0:T(8,128)S(1)}, f32[4,32,16,128]{3,2,1,0:T(8,128)}, u32[]{:S(2)}) copy-start(f32[4,32,16,128]{3,2,1,0:T(8,128)} %get-tuple-element.5) | copy-start | bytes 3145732
where the time goes:
time: 63.8 us; the launch traced here: 63.6 us
  Pallas kernels  59.6 us (93%)
  local copies, waits for them, and re-layouts  3.35 us (5%)
  between operations  0.65 us (1%)
    pallas_call x1, Pallas kernels, shards(): pl.pallas_call(functools.partial(kernel, counts, chunks), out_shape=(out,...  59.6 us
    unnamed x4, local copies, waits for them, and re-layouts  3.35 us

commit v1 on v0

--- a/solution.py
+++ b/solution.py
@@ -12,7 +12,7 @@
 LOW, HIGH = 0.25, 2.0
 ROUNDS = 9
 WIDTHS = (1, 3, 3, 3, 3, 4, 3, 3, 3)
-UNROLL = 4
+PAD = 8
 
 
 def cheb_constants():
@@ -28,8 +28,8 @@
 
 
 def kernel(counts, chunks, eta_hbm, force_hbm, sol_hbm, res_hbm,
-           e_ref, b_ref, f_ref, cx_ref, cym_ref, cyp_ref, czm_ref, czp_ref, dg_ref, inv_ref,
-           r_ref, x_ref, w0_ref, w1_ref, so_ref, ro_ref,
+           e_ref, b_ref, f_ref, cxm_ref, cxp_ref, cym_ref, cyp_ref, czm_ref, czp_ref, dg_ref, inv_ref,
+           r_ref, w0_ref, w1_ref, so_ref, ro_ref,
            sy_ref, hy_ref, sz_ref, hz_ref, ar_ref,
            in_sem, out_sem, xs_sem, xr_sem, ys_sem, yr_sem, zs_sem, zr_sem, as_sem, ar_sem):
     X, Y, Z = b_ref.shape[1:]
@@ -38,7 +38,7 @@
     nch = len(chunks)
     order = [0] + ([nch - 1] if nch > 1 else []) + list(range(1, nch - 1))
 
-    load_e = pltpu.make_async_copy(eta_hbm, e_ref.at[0, pl.ds(1, X)], in_sem.at[0])
+    load_e = pltpu.make_async_copy(eta_hbm, e_ref.at[0, pl.ds(1, X), pl.ds(PAD, Y)], in_sem.at[0])
     load_b = pltpu.make_async_copy(force_hbm, b_ref, in_sem.at[1])
     load_e.start()
     load_b.start()
@@ -70,7 +70,8 @@
         n = WIDTHS[k]
         face, halo = (X, 0) if side == 0 else (1, X + 1)
         return pltpu.make_async_remote_copy(
-            src_ref=field(k).at[pl.ds(0, n), face], dst_ref=field(k).at[pl.ds(0, n), halo],
+            src_ref=field(k).at[pl.ds(0, n), face, pl.ds(PAD, Y)],
+            dst_ref=field(k).at[pl.ds(0, n), halo, pl.ds(PAD, Y)],
             send_sem=xs_sem.at[k, side], recv_sem=xr_sem.at[k, side],
             device_id=target(0, side), device_id_type=MESH)
 
@@ -123,7 +124,7 @@
             zero = jnp.zeros((Y, Z), jnp.float32)
             for k in range(ROUNDS):
                 for c in range(WIDTHS[k]):
-                    field(k)[c, 0 if side == 0 else X + 1] = zero
+                    field(k)[c, 0 if side == 0 else X + 1, PAD:PAD + Y] = zero
         @pl.when(jnp.logical_not(receives(1, side)))
         def _():
             def body(k, carry):
@@ -137,24 +138,23 @@
                 return carry
             lax.fori_loop(0, ROUNDS, body, 0)
 
-    row = lax.broadcasted_iota(jnp.int32, (Y, Z), 0)
     lane = lax.broadcasted_iota(jnp.int32, (Y, Z), 1)
     blank = jnp.zeros((Y, Z), jnp.float32)
-    first_row, last_row, first_lane, last_lane = row == 0, row == Y - 1, lane == 0, lane == Z - 1
+    first_lane, last_lane = lane == 0, lane == Z - 1
 
     def neighbours(k, ch, c, x):
         f = field(k)
-        u = f[c, x + 1]
+        u = f[c, x + 1, PAD:PAD + Y]
         spot = c * X + x
-        ym = jnp.where(first_row, hy_ref[k, 0, c, pl.ds(x, 1)], pltpu.roll(u, 1, 0))
-        yp = jnp.where(last_row, hy_ref[k, 1, c, pl.ds(x, 1)], pltpu.roll(u, Y - 1, 0))
+        ym = f[c, x + 1, PAD - 1:PAD - 1 + Y]
+        yp = f[c, x + 1, PAD + 1:PAD + 1 + Y]
         zm = jnp.where(first_lane, pltpu.roll(hz_ref[k, 0, ch], lax.rem(Z - spot, Z), 1), pltpu.roll(u, 1, 1))
         zp = jnp.where(last_lane, pltpu.roll(hz_ref[k, 1, ch], Z - 1 - spot, 1), pltpu.roll(u, Z - 1, 1))
-        return u, f[c, x], f[c, x + 2], ym, yp, zm, zp
+        return u, f[c, x, PAD:PAD + Y], f[c, x + 2, PAD:PAD + Y], ym, yp, zm, zp
 
     def put(k, c, x, value, packs, store=True):
         if store:
-            field(k)[c, x + 1] = value
+            field(k)[c, x + 1, PAD:PAD + Y] = value
         sy_ref[k, 0, c, pl.ds(x, 1)] = value[Y - 1:Y]
         sy_ref[k, 1, c, pl.ds(x, 1)] = value[0:1]
         here = lane == c * X + x
@@ -163,12 +163,18 @@
 
     def sweep(need, make, body, extra=()):
         for ch in order:
+            lo, hi = chunks[ch]
             if need is not None:
                 wait_chunk(need, ch)
-            lo, hi = chunks[ch]
+                def rim(x, carry):
+                    for c in range(WIDTHS[need]):
+                        field(need)[c, x + 1, PAD - 1:PAD] = hy_ref[need, 0, c, pl.ds(x, 1)]
+                        field(need)[c, x + 1, PAD + Y:PAD + Y + 1] = hy_ref[need, 1, c, pl.ds(x, 1)]
+                    return carry
+                lax.fori_loop(lo, hi, rim, 0, unroll=hi - lo)
             def step(x, carry):
                 return body(ch, x, carry[0], carry[1])
-            packs, extra = lax.fori_loop(lo, hi, step, ((blank, blank), extra), unroll=UNROLL)
+            packs, extra = lax.fori_loop(lo, hi, step, ((blank, blank), extra), unroll=hi - lo)
             if make is not None:
                 sz_ref[make, 0, ch] = packs[0]
                 sz_ref[make, 1, ch] = packs[1]
@@ -177,7 +183,7 @@
 
     load_e.wait()
     pl.semaphore_wait(barrier, sum(counts) - 3)
-    sweep(None, 0, lambda ch, x, packs, extra: (put(0, 0, x, e_ref[0, x + 1], packs, False), extra))
+    sweep(None, 0, lambda ch, x, packs, extra: (put(0, 0, x, e_ref[0, x + 1, PAD:PAD + Y], packs, False), extra))
     load_b.wait()
 
     def setup(ch, x, packs, extra):
@@ -185,26 +191,26 @@
         cxm, cxp = 0.5 * (u + xm), 0.5 * (u + xp)
         cym, cyp = 0.5 * (u + ym), 0.5 * (u + yp)
         czm, czp = 0.5 * (u + zm), 0.5 * (u + zp)
-        cx_ref[x] = cxm
-        cx_ref[x + 1] = cxp
-        cym_ref[x], cyp_ref[x], czm_ref[x], czp_ref[x] = cym, cyp, czm, czp
         diagonal = cxp + cxm + cyp + cym + czp + czm
         inverse = 1.0 / diagonal
         dg_ref[x] = diagonal
         inv_ref[x] = inverse
+        cxm_ref[x], cxp_ref[x] = cxm * inverse, cxp * inverse
+        cym_ref[x], cyp_ref[x] = cym * inverse, cyp * inverse
+        czm_ref[x], czp_ref[x] = czm * inverse, czp * inverse
         for c in range(3):
-            packs = put(1, c, x, b_ref[c, x] * inverse / mid, packs)
+            packs = put(1, c, x, b_ref[c, x] * inverse * (1.0 / mid), packs)
         return packs, extra
 
     sweep(0, 1, setup)
 
-    def viscous(near, coef):
+    def coefs(x):
+        return (cxm_ref[x], cxp_ref[x], cym_ref[x], cyp_ref[x], czm_ref[x], czp_ref[x])
+
+    def scaled(near, coef):
         u, xm, xp, ym, yp, zm, zp = near
-        cxm, cxp, cym, cyp, czm, czp, dg = coef
-        return dg * u - cxp * xp - cxm * xm - cyp * yp - cym * ym - czp * zp - czm * zm
-
-    def coefs(x):
-        return (cx_ref[x], cx_ref[x + 1], cym_ref[x], cyp_ref[x], czm_ref[x], czp_ref[x], dg_ref[x])
+        cxm, cxp, cym, cyp, czm, czp = coef
+        return u - ((cxp * xp + cxm * xm) + (cyp * yp + cym * ym) + (czp * zp + czm * zm))
 
     def smooth(base, forcing, at, shift=None):
         keep, gain = steps[at]
@@ -212,20 +218,20 @@
         last = at == SWEEPS - 1
 
         def body(ch, x, packs, extra):
-            coef, inverse = coefs(x), inv_ref[x]
+            coef = coefs(x)
+            inverse = inv_ref[x] if at == 0 else None
             for c in range(3):
                 near = neighbours(src, ch, c, x)
-                r = (forcing[c, x] if at == 0 else r_ref[c, x]) - viscous(near, coef)
-                d = keep * near[0] + gain * r * inverse
-                total = (near[0] if at == 0 else x_ref[c, x]) + d
+                r = (forcing[c, x] * inverse if at == 0 else r_ref[c, x]) - scaled(near, coef)
+                d = keep * near[0] + gain * r
                 if last:
+                    for k in range(base, dst):
+                        d = d + (near[0] if k == src else field(k)[c, x + 1, PAD:PAD + Y])
                     if shift is not None:
-                        total = total - shift * f_ref[base - 2, c, x + 1]
-                    packs = put(dst, c, x, total, packs)
+                        d = d - shift * f_ref[base - 2, c, x + 1, PAD:PAD + Y]
                 else:
                     r_ref[c, x] = r
-                    x_ref[c, x] = total
-                    packs = put(dst, c, x, d, packs)
+                packs = put(dst, c, x, d, packs)
             return packs, extra
 
         sweep(src, dst, body)
@@ -278,17 +284,18 @@
 
     def stokes0(ch, x, packs, sums):
         bb, wb, ww = sums
-        coef, inverse = coefs(x), inv_ref[x]
+        coef, diagonal = coefs(x), dg_ref[x]
         near = [neighbours(4, ch, c, x) for c in range(3)]
         for c in range(3):
-            w, b = viscous(near[c], coef), b_ref[c, x]
+            part, b = scaled(near[c], coef), b_ref[c, x]
+            w = diagonal * part
             bb, wb, ww = bb + b * b, wb + w * b, ww + w * w
             w0_ref[c, x] = w
-            packs = put(5, c, x, w * inverse / mid, packs)
+            packs = put(5, c, x, part * (1.0 / mid), packs)
         div = -0.5 * (near[0][2] - near[0][1] + (near[1][4] - near[1][3]) + (near[2][6] - near[2][5]))
         ww = ww + div * div
         w0_ref[3, x] = div
-        packs = put(5, 3, x, e_ref[0, x + 1] * div, packs)
+        packs = put(5, 3, x, e_ref[0, x + 1, PAD:PAD + Y] * div, packs)
         return packs, (bb, wb, ww)
 
     sums = sweep(4, 5, stokes0, (blank, blank, blank))
@@ -305,12 +312,12 @@
 
     def stokes1(ch, x, packs, sums):
         wb, wu, ww = sums
-        coef = coefs(x)
+        coef, diagonal = coefs(x), dg_ref[x]
         near = [neighbours(8, ch, c, x) for c in range(3)]
         _, pxm, pxp, pym, pyp, pzm, pzp = neighbours(5, ch, 3, x)
         grads = (0.5 * (pxp - pxm), 0.5 * (pyp - pym), 0.5 * (pzp - pzm))
         for c in range(3):
-            w, b = viscous(near[c], coef) + grads[c], b_ref[c, x]
+            w, b = diagonal * scaled(near[c], coef) + grads[c], b_ref[c, x]
             u = w0_ref[c, x] - h00 * b
             wb, wu, ww = wb + w * b, wu + w * u, ww + w * w
             w1_ref[c, x] = w
@@ -355,12 +362,12 @@
         def body(x, carry):
             for c in range(3):
                 b = b_ref[c, x]
-                so_ref[c, x] = z0_weight * f_ref[3, c, x + 1] + z1_weight * f_ref[7, c, x + 1]
+                so_ref[c, x] = z0_weight * f_ref[3, c, x + 1, PAD:PAD + Y] + z1_weight * f_ref[7, c, x + 1, PAD:PAD + Y]
                 ro_ref[c, x] = b_weight * b + u_weight * (w0_ref[c, x] - h00 * b) + w_weight * w1_ref[c, x]
-            so_ref[3, x] = z1_weight * f_ref[4, 3, x + 1]
+            so_ref[3, x] = z1_weight * f_ref[4, 3, x + 1, PAD:PAD + Y]
             ro_ref[3, x] = u_weight * w0_ref[3, x] + w_weight * w1_ref[3, x]
             return carry
-        lax.fori_loop(*chunks[ch], body, 0, unroll=UNROLL)
+        lax.fori_loop(*chunks[ch], body, 0, unroll=4)
         for copy in out_copies(ch):
             copy.start()
 
@@ -402,10 +409,10 @@
         dma = pltpu.SemaphoreType.DMA
         spots = sum(counts)
         scratch = [
-            pltpu.VMEM((1, X + 2, Y, Z), f32), pltpu.VMEM((3, X, Y, Z), f32),
-            pltpu.VMEM((ROUNDS - 1, 4, X + 2, Y, Z), f32), pltpu.VMEM((X + 1, Y, Z), f32),
-            block, block, block, block, block, block,
-            pltpu.VMEM((3, X, Y, Z), f32), pltpu.VMEM((3, X, Y, Z), f32),
+            pltpu.VMEM((1, X + 2, Y + 2 * PAD, Z), f32), pltpu.VMEM((3, X, Y, Z), f32),
+            pltpu.VMEM((ROUNDS - 1, 4, X + 2, Y + 2 * PAD, Z), f32),
+            block, block, block, block, block, block, block, block,
+            pltpu.VMEM((3, X, Y, Z), f32),
             pltpu.VMEM((4, X, Y, Z), f32), pltpu.VMEM((4, X, Y, Z), f32),
             pltpu.VMEM((4, X, Y, Z), f32), pltpu.VMEM((4, X, Y, Z), f32),
             pltpu.VMEM((ROUNDS, 2, 4, X, Z), f32), pltpu.VMEM((ROUNDS, 2, 4, X, Z), f32),

time: 63.8 us -> 78.8 us (1.24)
  Pallas kernels: 59.6 us -> 74.6 us
    pallas_call x1, Pallas kernels: 59.6 us -> 74.6 us  [shards(): pl.pallas_call(functools.partial(kernel, counts, chunks), out_shape=(out,...]
where the time goes in v1:
time: 78.8 us; the launch traced here: 78.6 us
  Pallas kernels  74.6 us (95%)
  local copies, waits for them, and re-layouts  3.35 us (4%)
    pallas_call x1, Pallas kernels, shards(): pl.pallas_call(functools.partial(kernel, counts, chunks), out_shape=(out,...  74.6 us
    unnamed x4, local copies, waits for them, and re-layouts  3.35 us

profile of v1, /device:TPU:0, one launch (start us, length us, event | category | flops | bytes accessed | tf_op | source)
XLA Modules:
  0.0 78.6 jit_solution(2578244015916108447)
XLA Ops:
  0.6 74.6 %fgmres.1 = (f32[4,32,16,128]{3,2,1,0:T(8,128)}, f32[4,32,16,128]{3,2,1,0:T(8,128)}) custom-call(f32[32,16,128]{2,1,0:T(8,128)} %eta_hbm.1, f32[3,32,16,128]{3,2,1,0:T(8,128)} %force_hbm.1), custom_call_target="tpu_custom_call" | custom-call | tf_op jit(solution)/shard_map/fgmres/pallas_call | solution.py:427
  75.2 0.0 copy-start
  75.2 2.4 %copy.6 = f32[4,32,16,128]{3,2,1,0:T(8,128)} copy(f32[4,32,16,128]{3,2,1,0:T(8,128)} %get-tuple-element.4) | data formatting | bytes 2097152
  77.6 0.0 copy-done
  77.6 1.0 %copy.7 = f32[4,32,16,128]{3,2,1,0:T(8,128)} copy(f32[4,32,16,128]{3,2,1,0:T(8,128)S(1)} %copy-done) | data formatting | bytes 2097152
Async XLA Ops:
  75.2 2.4 %copy-start = (f32[4,32,16,128]{3,2,1,0:T(8,128)S(1)}, f32[4,32,16,128]{3,2,1,0:T(8,128)}, u32[]{:S(2)}) copy-start(f32[4,32,16,128]{3,2,1,0:T(8,128)} %get-tuple-element.5) | copy-start | bytes 3145732

commit v2 on v1

--- a/solution.py
+++ b/solution.py
@@ -12,6 +12,7 @@
 LOW, HIGH = 0.25, 2.0
 ROUNDS = 9
 WIDTHS = (1, 3, 3, 3, 3, 4, 3, 3, 3)
+UNROLL = 4
 PAD = 8
 
 
@@ -35,8 +36,7 @@
     X, Y, Z = b_ref.shape[1:]
     mid, steps = cheb_constants()
     me = [lax.axis_index(a) for a in AXES]
-    nch = len(chunks)
-    order = [0] + ([nch - 1] if nch > 1 else []) + list(range(1, nch - 1))
+    size, nch = chunks
 
     load_e = pltpu.make_async_copy(eta_hbm, e_ref.at[0, pl.ds(1, X), pl.ds(PAD, Y)], in_sem.at[0])
     load_b = pltpu.make_async_copy(force_hbm, b_ref, in_sem.at[1])
@@ -77,10 +77,10 @@
 
     def y_copy(k, side, ch):
         n = WIDTHS[k]
-        lo, hi = chunks[ch]
+        span = pl.ds(pl.multiple_of(ch * size, size), size)
         return pltpu.make_async_remote_copy(
-            src_ref=sy_ref.at[k, side, pl.ds(0, n), pl.ds(lo, hi - lo)],
-            dst_ref=hy_ref.at[k, side, pl.ds(0, n), pl.ds(lo, hi - lo)],
+            src_ref=sy_ref.at[k, side, pl.ds(0, n), span],
+            dst_ref=hy_ref.at[k, side, pl.ds(0, n), span],
             send_sem=ys_sem.at[k, side, ch], recv_sem=yr_sem.at[k, side, ch],
             device_id=target(1, side), device_id_type=MESH)
 
@@ -99,10 +99,9 @@
             def _():
                 z_copy(k, side, ch).start()
         for side, edge in ((0, nch - 1), (1, 0)):
-            if ch == edge:
-                @pl.when(sends(0, side))
-                def _():
-                    x_copy(k, side).start()
+            @pl.when(jnp.logical_and(ch == edge, sends(0, side)))
+            def _():
+                x_copy(k, side).start()
 
     def wait_chunk(k, ch):
         for side in (0, 1):
@@ -113,10 +112,9 @@
             def _():
                 z_copy(k, side, ch).wait_recv()
         for side, edge in ((0, 0), (1, nch - 1)):
-            if ch == edge:
-                @pl.when(receives(0, side))
-                def _():
-                    x_copy(k, side).wait_recv()
+            @pl.when(jnp.logical_and(ch == edge, receives(0, side)))
+            def _():
+                x_copy(k, side).wait_recv()
 
     for side in (0, 1):
         @pl.when(jnp.logical_not(receives(0, side)))
@@ -152,41 +150,49 @@
         zp = jnp.where(last_lane, pltpu.roll(hz_ref[k, 1, ch], Z - 1 - spot, 1), pltpu.roll(u, Z - 1, 1))
         return u, f[c, x, PAD:PAD + Y], f[c, x + 2, PAD:PAD + Y], ym, yp, zm, zp
 
-    def put(k, c, x, value, packs, store=True):
+    def put(k, c, x, value, store=True):
         if store:
             field(k)[c, x + 1, PAD:PAD + Y] = value
         sy_ref[k, 0, c, pl.ds(x, 1)] = value[Y - 1:Y]
         sy_ref[k, 1, c, pl.ds(x, 1)] = value[0:1]
-        here = lane == c * X + x
-        return (jnp.where(here, jnp.broadcast_to(value[:, Z - 1:Z], (Y, Z)), packs[0]),
-                jnp.where(here, jnp.broadcast_to(value[:, 0:1], (Y, Z)), packs[1]))
 
     def sweep(need, make, body, extra=()):
-        for ch in order:
-            lo, hi = chunks[ch]
+        def chunk(i, extra):
+            ch = lax.rem(i * (nch - 1), nch)
+            lo = pl.multiple_of(ch * size, size)
             if need is not None:
                 wait_chunk(need, ch)
-                def rim(x, carry):
-                    for c in range(WIDTHS[need]):
-                        field(need)[c, x + 1, PAD - 1:PAD] = hy_ref[need, 0, c, pl.ds(x, 1)]
-                        field(need)[c, x + 1, PAD + Y:PAD + Y + 1] = hy_ref[need, 1, c, pl.ds(x, 1)]
-                    return carry
-                lax.fori_loop(lo, hi, rim, 0, unroll=hi - lo)
-            def step(x, carry):
-                return body(ch, x, carry[0], carry[1])
-            packs, extra = lax.fori_loop(lo, hi, step, ((blank, blank), extra), unroll=hi - lo)
+                for c in range(WIDTHS[need]):
+                    low, high = hy_ref[need, 0, c, pl.ds(lo, size)], hy_ref[need, 1, c, pl.ds(lo, size)]
+                    for j in range(size):
+                        field(need)[c, lo + j + 1, PAD - 1:PAD] = low[j:j + 1]
+                        field(need)[c, lo + j + 1, PAD + Y:PAD + Y + 1] = high[j:j + 1]
+            extra = lax.fori_loop(0, size, lambda j, extra: body(ch, lo + j, extra), extra, unroll=UNROLL)
             if make is not None:
-                sz_ref[make, 0, ch] = packs[0]
-                sz_ref[make, 1, ch] = packs[1]
+                low = high = blank
+                for j in range(size):
+                    for c in range(WIDTHS[make]):
+                        spot = c * X + lo + j
+                        here = lane == spot
+                        value = field(make)[c, lo + j + 1, PAD:PAD + Y]
+                        low = jnp.where(here, pltpu.roll(value, lax.rem(spot + 1, Z), 1), low)
+                        high = jnp.where(here, pltpu.roll(value, spot, 1), high)
+                sz_ref[make, 0, ch] = low
+                sz_ref[make, 1, ch] = high
                 start_chunk(make, ch)
-        return extra
+            return extra
+        return lax.fori_loop(0, nch, chunk, extra)
 
     load_e.wait()
     pl.semaphore_wait(barrier, sum(counts) - 3)
-    sweep(None, 0, lambda ch, x, packs, extra: (put(0, 0, x, e_ref[0, x + 1, PAD:PAD + Y], packs, False), extra))
+    def first(ch, x, extra):
+        put(0, 0, x, e_ref[0, x + 1, PAD:PAD + Y], False)
+        return extra
+
+    sweep(None, 0, first)
     load_b.wait()
 
-    def setup(ch, x, packs, extra):
+    def setup(ch, x, extra):
         u, xm, xp, ym, yp, zm, zp = neighbours(0, ch, 0, x)
         cxm, cxp = 0.5 * (u + xm), 0.5 * (u + xp)
         cym, cyp = 0.5 * (u + ym), 0.5 * (u + yp)
@@ -199,8 +205,8 @@
         cym_ref[x], cyp_ref[x] = cym * inverse, cyp * inverse
         czm_ref[x], czp_ref[x] = czm * inverse, czp * inverse
         for c in range(3):
-            packs = put(1, c, x, b_ref[c, x] * inverse * (1.0 / mid), packs)
-        return packs, extra
+            put(1, c, x, b_ref[c, x] * inverse * (1.0 / mid))
+        return extra
 
     sweep(0, 1, setup)
 
@@ -217,7 +223,7 @@
         src, dst = base + at, base + at + 1
         last = at == SWEEPS - 1
 
-        def body(ch, x, packs, extra):
+        def body(ch, x, extra):
             coef = coefs(x)
             inverse = inv_ref[x] if at == 0 else None
             for c in range(3):
@@ -231,8 +237,8 @@
                         d = d - shift * f_ref[base - 2, c, x + 1, PAD:PAD + Y]
                 else:
                     r_ref[c, x] = r
-                packs = put(dst, c, x, d, packs)
-            return packs, extra
+                put(dst, c, x, d)
+            return extra
 
         sweep(src, dst, body)
 
@@ -282,7 +288,7 @@
     for at in range(SWEEPS):
         smooth(1, b_ref, at)
 
-    def stokes0(ch, x, packs, sums):
+    def stokes0(ch, x, sums):
         bb, wb, ww = sums
         coef, diagonal = coefs(x), dg_ref[x]
         near = [neighbours(4, ch, c, x) for c in range(3)]
@@ -291,12 +297,12 @@
             w = diagonal * part
             bb, wb, ww = bb + b * b, wb + w * b, ww + w * w
             w0_ref[c, x] = w
-            packs = put(5, c, x, part * (1.0 / mid), packs)
+            put(5, c, x, part * (1.0 / mid))
         div = -0.5 * (near[0][2] - near[0][1] + (near[1][4] - near[1][3]) + (near[2][6] - near[2][5]))
         ww = ww + div * div
         w0_ref[3, x] = div
-        packs = put(5, 3, x, e_ref[0, x + 1, PAD:PAD + Y] * div, packs)
-        return packs, (bb, wb, ww)
+        put(5, 3, x, e_ref[0, x + 1, PAD:PAD + Y] * div)
+        return (bb, wb, ww)
 
     sums = sweep(4, 5, stokes0, (blank, blank, blank))
     ar_start(0, 0, tile_of(sums))
@@ -310,7 +316,7 @@
     h10 = jnp.sqrt(ww / square - h00 * h00)
     smooth(5, w0_ref, 2, h00)
 
-    def stokes1(ch, x, packs, sums):
+    def stokes1(ch, x, sums):
         wb, wu, ww = sums
         coef, diagonal = coefs(x), dg_ref[x]
         near = [neighbours(8, ch, c, x) for c in range(3)]
@@ -324,7 +330,7 @@
         div = -0.5 * (near[0][2] - near[0][1] + (near[1][4] - near[1][3]) + (near[2][6] - near[2][5]))
         wu, ww = wu + div * w0_ref[3, x], ww + div * div
         w1_ref[3, x] = div
-        return packs, (wb, wu, ww)
+        return (wb, wu, ww)
 
     sums = sweep(8, None, stokes1, (blank, blank, blank))
     ar_start(1, 0, tile_of(sums))
@@ -353,23 +359,33 @@
     w_weight = c2 / (h21 * beta * h10)
 
     def out_copies(ch):
-        lo, hi = chunks[ch]
-        span = pl.ds(lo, hi - lo)
+        span = pl.ds(ch * size, size)
         return (pltpu.make_async_copy(so_ref.at[:, span], sol_hbm.at[:, span], out_sem.at[0, ch]),
                 pltpu.make_async_copy(ro_ref.at[:, span], res_hbm.at[:, span], out_sem.at[1, ch]))
 
-    for ch in range(nch):
-        def body(x, carry):
+    def finish(ch, carry):
+        def body(j, carry):
+            x = ch * size + j
             for c in range(3):
                 b = b_ref[c, x]
-                so_ref[c, x] = z0_weight * f_ref[3, c, x + 1, PAD:PAD + Y] + z1_weight * f_ref[7, c, x + 1, PAD:PAD + Y]
+                so_ref[c, x] = (z0_weight * f_ref[3, c, x + 1, PAD:PAD + Y]
+                                + z1_weight * f_ref[7, c, x + 1, PAD:PAD + Y])
                 ro_ref[c, x] = b_weight * b + u_weight * (w0_ref[c, x] - h00 * b) + w_weight * w1_ref[c, x]
             so_ref[3, x] = z1_weight * f_ref[4, 3, x + 1, PAD:PAD + Y]
             ro_ref[3, x] = u_weight * w0_ref[3, x] + w_weight * w1_ref[3, x]
             return carry
-        lax.fori_loop(*chunks[ch], body, 0, unroll=4)
+        lax.fori_loop(0, size, body, 0, unroll=UNROLL)
         for copy in out_copies(ch):
             copy.start()
+        return carry
+
+    lax.fori_loop(0, nch, finish, 0)
+
+    def each_chunk(act):
+        def body(ch, carry):
+            act(ch)
+            return carry
+        lax.fori_loop(0, nch, body, 0)
 
     for side in (0, 1):
         @pl.when(sends(0, side))
@@ -379,20 +395,16 @@
         @pl.when(sends(1, side))
         def _():
             for k in range(ROUNDS):
-                for ch in range(nch):
-                    y_copy(k, side, ch).wait_send()
+                each_chunk(lambda ch: y_copy(k, side, ch).wait_send())
         @pl.when(sends(2, side))
         def _():
             for k in range(ROUNDS):
-                for ch in range(nch):
-                    z_copy(k, side, ch).wait_send()
+                each_chunk(lambda ch: z_copy(k, side, ch).wait_send())
     for which in (0, 1):
         for stage in range(3):
             for off in range(1, counts[stages[stage]]):
                 ar_copy(which, stage, off).wait_send()
-    for ch in range(nch):
-        for copy in out_copies(ch):
-            copy.wait()
+    each_chunk(lambda ch: [copy.wait() for copy in out_copies(ch)])
 
 
 def solution(mesh):
@@ -402,8 +414,8 @@
         X, Y, Z = viscosity.shape
         assert 4 * X <= Z
         size = 8 if X % 8 == 0 else X
-        chunks = tuple((lo, lo + size) for lo in range(0, X, size))
-        nch = len(chunks)
+        nch = X // size
+        chunks = (size, nch)
         f32 = jnp.float32
         block = pltpu.VMEM((X, Y, Z), f32)
         dma = pltpu.SemaphoreType.DMA

time: 78.8 us -> 60.1 us (0.76)
  Pallas kernels: 74.6 us -> 56 us
    pallas_call x1, Pallas kernels: 74.6 us -> 56 us  [shards(): pl.pallas_call(functools.partial(kernel, counts, chunks), out_shape=(out,...]
where the time goes in v2:
time: 60.1 us; the launch traced here: 59.9 us
  Pallas kernels  56 us (93%)
  local copies, waits for them, and re-layouts  3.35 us (6%)
  between operations  0.65 us (1%)
    pallas_call x1, Pallas kernels, shards(): pl.pallas_call(functools.partial(kernel, counts, chunks), out_shape=(out,...  56 us
    unnamed x4, local copies, waits for them, and re-layouts  3.35 us

profile of v2, /device:TPU:0, one launch (start us, length us, event | category | flops | bytes accessed | tf_op | source)
XLA Modules:
  0.0 59.9 jit_solution(17888356322819870104)
XLA Ops:
  0.6 56.0 %fgmres.1 = (f32[4,32,16,128]{3,2,1,0:T(8,128)}, f32[4,32,16,128]{3,2,1,0:T(8,128)}) custom-call(f32[32,16,128]{2,1,0:T(8,128)} %eta_hbm.1, f32[3,32,16,128]{3,2,1,0:T(8,128)} %force_hbm.1), custom_call_target="tpu_custom_call" | custom-call | tf_op jit(solution)/shard_map/fgmres/pallas_call | solution.py:439
  56.6 0.0 copy-start
  56.6 2.4 %copy.6 = f32[4,32,16,128]{3,2,1,0:T(8,128)} copy(f32[4,32,16,128]{3,2,1,0:T(8,128)} %get-tuple-element.4) | data formatting | bytes 2097152
  59.0 0.0 copy-done
  59.0 1.0 %copy.7 = f32[4,32,16,128]{3,2,1,0:T(8,128)} copy(f32[4,32,16,128]{3,2,1,0:T(8,128)S(1)} %copy-done) | data formatting | bytes 2097152
Async XLA Ops:
  56.6 2.4 %copy-start = (f32[4,32,16,128]{3,2,1,0:T(8,128)S(1)}, f32[4,32,16,128]{3,2,1,0:T(8,128)}, u32[]{:S(2)}) copy-start(f32[4,32,16,128]{3,2,1,0:T(8,128)} %get-tuple-element.5) | copy-start | bytes 3145732

commit v3 on v2

--- a/solution.py
+++ b/solution.py
@@ -12,7 +12,7 @@
 LOW, HIGH = 0.25, 2.0
 ROUNDS = 9
 WIDTHS = (1, 3, 3, 3, 3, 4, 3, 3, 3)
-UNROLL = 4
+UNROLL = 8
 PAD = 8
 
 

time: 60.1 us -> 58.1 us (0.967)
  Pallas kernels: 56 us -> 54 us
    pallas_call x1, Pallas kernels: 56 us -> 54 us  [shards(): pl.pallas_call(functools.partial(kernel, counts, chunks), out_shape=(out,...]
where the time goes in v3:
time: 58.1 us; the launch traced here: 58 us
  Pallas kernels  54 us (93%)
  local copies, waits for them, and re-layouts  3.35 us (6%)
  between operations  0.65 us (1%)
    pallas_call x1, Pallas kernels, shards(): pl.pallas_call(functools.partial(kernel, counts, chunks), out_shape=(out,...  54 us
    unnamed x4, local copies, waits for them, and re-layouts  3.35 us

profile of v3, /device:TPU:0, one launch (start us, length us, event | category | flops | bytes accessed | tf_op | source)
XLA Modules:
  0.0 58.0 jit_solution(8487032167012520359)
XLA Ops:
  0.6 54.0 %fgmres.1 = (f32[4,32,16,128]{3,2,1,0:T(8,128)}, f32[4,32,16,128]{3,2,1,0:T(8,128)}) custom-call(f32[32,16,128]{2,1,0:T(8,128)} %eta_hbm.1, f32[3,32,16,128]{3,2,1,0:T(8,128)} %force_hbm.1), custom_call_target="tpu_custom_call" | custom-call | tf_op jit(solution)/shard_map/fgmres/pallas_call | solution.py:439
  54.6 0.0 copy-start
  54.6 2.4 %copy.6 = f32[4,32,16,128]{3,2,1,0:T(8,128)} copy(f32[4,32,16,128]{3,2,1,0:T(8,128)} %get-tuple-element.4) | data formatting | bytes 2097152
  57.0 0.0 copy-done
  57.0 1.0 %copy.7 = f32[4,32,16,128]{3,2,1,0:T(8,128)} copy(f32[4,32,16,128]{3,2,1,0:T(8,128)S(1)} %copy-done) | data formatting | bytes 2097152
Async XLA Ops:
  54.6 2.4 %copy-start = (f32[4,32,16,128]{3,2,1,0:T(8,128)S(1)}, f32[4,32,16,128]{3,2,1,0:T(8,128)}, u32[]{:S(2)}) copy-start(f32[4,32,16,128]{3,2,1,0:T(8,128)} %get-tuple-element.5) | copy-start | bytes 3145732
